TPU v7x, 256 devices: a whole 4x4x8 slice. The times are simulated.
256 devices in a mesh: gz: 8 (over x, core), gx: 32 (over z, y).
Axes of the slice: x: 4, y: 4, z: 8, core: 2. Of those that a mesh axis runs over, the one named last changes fastest.
Arguments:
- volume: float32 [256, 512, 256], P('gz', 'gx')
- measured: float32 [2, 256, 2048], P(None, 'gz')
- weight_blocks: bfloat16 [64, 128, 128], replicated, may hold values from 0 to 2
- view_order: int32 [2], replicated, may hold values from 0 to 1, each once
- tile_voxel: int32 [2, 8, 16384], P(None, 'gz', 'gx'), may hold values from 0 to 1023
- tile_column: int32 [2, 8, 16384], P(None, 'gz', 'gx'), may hold values from 0 to 15
- tile_block: int32 [2, 8, 16384], P(None, 'gz', 'gx'), may hold values from 0 to 63
- entry_count: int32 [2, 8, 32], P(None, 'gz', 'gx'), may hold values from 1 to 512, as said below
Outputs:
- volume_out: float32 [256, 512, 256], P('gz', 'gx')
Inputs may be any that keep to these rules, and one draw needn't show every extreme that they name: Entries of block (a, c) of view v at or past entry_count[v, a, c] are not used; in every view some block has 512 live entries.
All inputs are finite; a program needn't handle non-finite values.
Results may differ from a plain program's by a relative error of at most 0.0027.
Values may be sent and summed in bfloat16 or wider, within the bound.
A program may use at most 64 MiB of HBM per device.

v0:
```python
import jax
import jax.numpy as jnp
from jax import lax
from jax.sharding import PartitionSpec as P

TV_STEPS = 4
smooth_floor = 0.01
step_gain = 0.25
norm_floor = 1e-06
group_rows = 128


def padded_2(cells, sides, width):
    for axis, dim in sides:
        count = lax.axis_size(axis)
        ends = count - 1
        head = lax.slice_in_dim(cells, 0, width, axis=dim)
        tail = lax.slice_in_dim(cells, cells.shape[dim] - width, cells.shape[dim], axis=dim)
        cells = jnp.concatenate(
            [
                lax.ppermute(tail, axis, [(i, (i + 1) % count) for i in range(ends)]),
                cells,
                lax.ppermute(head, axis, [((i + 1) % count, i) for i in range(ends)]),
            ],
            axis=dim,
        )
    return cells


def tv_grad(padded):
    base_cells = padded[:-1, :-1, :-1]
    diff_z = padded[1:, :-1, :-1] - base_cells
    diff_x = padded[:-1, 1:, :-1] - base_cells
    diff_y = padded[:-1, :-1, 1:] - base_cells
    inverse = lax.rsqrt(diff_z * diff_z + diff_x * diff_x + diff_y * diff_y + smooth_floor)
    flow_z = diff_z * inverse
    flow_x = diff_x * inverse
    flow_y = diff_y * inverse
    flow_all = flow_z + flow_x + flow_y
    return flow_z[:-1, 1:, 1:] + flow_x[1:, :-1, 1:] + flow_y[1:, 1:, :-1] - flow_all[1:, 1:, 1:]


def pad_depth(field):
    return jnp.pad(field, ((0, 0), (0, 0), (1, 1)))


def body(
    volume, measured, weight_blocks, view_order, tile_voxel, tile_column, tile_block, entry_count
):
    depth_z, depth_x, depth_y = volume.shape
    tiles_y = depth_y // group_rows
    tiles_u = measured.shape[2] // group_rows
    slab_tiles = depth_z * tiles_u
    plane_tiles = depth_x * tiles_y
    row_weight = jnp.sum(weight_blocks, axis=2, dtype=jnp.float32)
    col_weight = jnp.sum(weight_blocks, axis=1, dtype=jnp.float32)
    offsets = jnp.arange(group_rows, dtype=jnp.int32)
    current = volume
    for turn_index in range(view_order.shape[0]):
        view_index = view_order[turn_index]
        voxel_list = lax.dynamic_index_in_dim(tile_voxel, view_index, 0, keepdims=False)[0]
        column_list = lax.dynamic_index_in_dim(tile_column, view_index, 0, keepdims=False)[0]
        block_list = lax.dynamic_index_in_dim(tile_block, view_index, 0, keepdims=False)[0]
        live_count = lax.dynamic_index_in_dim(entry_count, view_index, 0, keepdims=False)[0, 0]
        rounds = (live_count + group_rows - 1) // group_rows
        voxel_tiles = current.astype(jnp.bfloat16).reshape(-1, group_rows)

        def gather_group(index):
            begin = index * group_rows
            voxels = lax.dynamic_slice_in_dim(voxel_list, begin, group_rows)
            columns = lax.dynamic_slice_in_dim(column_list, begin, group_rows)
            chosen = lax.dynamic_slice_in_dim(block_list, begin, group_rows)
            weight = (begin + offsets < live_count).astype(jnp.float32)[:, None]
            detector = voxels // plane_tiles * tiles_u + columns
            return (voxels, detector, chosen, weight)

        def forward(index, carry):
            projection, ray_sum = carry
            voxels, detector, chosen, weight = gather_group(index)
            product = jnp.einsum(
                "ejk,ek->ej",
                weight_blocks[chosen],
                voxel_tiles[voxels],
                preferred_element_type=jnp.float32,
            )
            return (
                projection.at[detector].add(product * weight),
                ray_sum.at[detector].add(row_weight[chosen] * weight),
            )

        empty = jnp.zeros((slab_tiles, group_rows), jnp.float32)
        projection, ray_sum = lax.fori_loop(0, rounds, forward, (empty, empty))
        target = lax.dynamic_index_in_dim(measured, view_index, 0, keepdims=False).reshape(
            slab_tiles, group_rows
        )
        projection, ray_sum = (
            lax.psum(projection.astype(jnp.bfloat16), "gx").astype(jnp.float32),
            lax.psum(ray_sum.astype(jnp.bfloat16), "gx").astype(jnp.float32),
        )
        residual = ((target - projection) / (ray_sum + 1.0)).astype(jnp.bfloat16)

        def backward(index, carry):
            change, voxel_sum = carry
            voxels, detector, chosen, weight = gather_group(index)
            product = jnp.einsum(
                "ejk,ej->ek",
                weight_blocks[chosen],
                residual[detector],
                preferred_element_type=jnp.float32,
            )
            return (
                change.at[voxels].add(product * weight),
                voxel_sum.at[voxels].add(col_weight[chosen] * weight),
            )

        blank = jnp.zeros((voxel_tiles.shape[0], group_rows), jnp.float32)
        change, voxel_sum = lax.fori_loop(0, rounds, backward, (blank, blank))
        current = current + (change / (voxel_sum + 1.0)).reshape(current.shape)
    art_volume = jnp.maximum(current, 0.0)
    difference = art_volume - volume
    change_part = jnp.sum(difference * difference)
    change_total = None
    change_total = lax.psum(change_part, ("gz", "gx"))
    smooth = art_volume
    for sweep_index in range(TV_STEPS):
        padded = padded_2(smooth, (("gz", 0), ("gx", 1)), 1)
        slope = tv_grad(pad_depth(padded))
        slope_part = jnp.sum(slope * slope)
        if sweep_index == 0:
            slope_total = lax.psum(slope_part, ("gz", "gx"))
        else:
            slope_total = lax.psum(slope_part, ("gz", "gx"))
        change_total, scale_now = (
            change_total,
            step_gain * jnp.sqrt(change_total) / jnp.sqrt(slope_total + norm_floor),
        )
        smooth = smooth - scale_now * slope
    return smooth


def solution(mesh):
    return jax.shard_map(
        body,
        mesh=mesh,
        in_specs=(
            P("gz", "gx", None),
            P(None, "gz", None),
            P(),
            P(),
            P(None, "gz", "gx"),
            P(None, "gz", "gx"),
            P(None, "gz", "gx"),
            P(None, "gz", "gx"),
        ),
        out_specs=P("gz", "gx", None),
        check_vma=False,
    )
```

profile of v0, /device:TPU:1, one launch (start us, length us, event | category | flops | bytes accessed | tf_op | source)
XLA Modules:
  0.0 943.3 jit_solution(2549535672975663778)
XLA Ops:
  14.3 2.4 convert_reduce_fusion
  17.6 13.5 %while.60 = (s32[]{:T(128)}, f32[512,128]{1,0:T(8,128)S(1)}, f32[512,128]{1,0:T(8,128)}, s32[]{:T(128)}, s32[512]{0:T(512)S(1)}, /*index=5*/s32[512]{0:T(512)S(1...) while((s32[]{:T(128)}, f32[512,128]{1,0:T(8,128)S(1)}, ...), condition=%wide.region_4.5_spmd.clone, body=%wide.region_1.4_spmd.clone.sunk | while | flops 4265478 | bytes 13388487 | solution.py:92
  17.7 3.0 gather_fusion
  21.5 4.4 fusion.99
  28.1 3.1 scatter_custom_fusion.43
  31.8 1.6 convert_element_type.89
  36.0 180.4 %all-reduce.12.cloned.1.call-done = (bf16[512,128]{1,0:T(8,128)(2,1)}, bf16[512,128]{1,0:T(8,128)(2,1)}) async-done(((bf16[512,128]{1,0:T(8,128)(2,1)}, bf16[512,128]{1,0:T(8,128)(2,1)}), (bf16[512,128]{1,0:T(8,128)(2,1)}, bf16[512,128]{1,0:T(8,128)(2,1)})) %all-reduce.12.cloned.1.call-update) | async-done | bytes 262160 | tf_op jit(solution)/shard_map/psum | solution.py:98
  219.1 14.2 %while.61 = (s32[]{:T(128)}, f32[1024,128]{1,0:T(8,128)}, f32[1024,128]{1,0:T(8,128)}, s32[]{:T(128)}, s32[512]{0:T(512)S(1)}, /*index=5*/s32[512]{0:T(512)S(1)}...) while((s32[]{:T(128)}, f32[1024,128]{1,0:T(8,128)}, ...), condition=%wide.region_11.12_spmd.clone, body=%wide.region_8.11_spmd.clone.sunk | while | flops 4265478 | bytes 13912775 | solution.py:117
  219.2 3.0 gather_fusion.2
  223.0 3.4 fusion.104
  227.0 3.1 scatter_custom_fusion.46
  230.1 3.3 scatter_custom_fusion.47
  233.4 2.1 add_divide_fusion.1
  235.4 2.0 reshape.54
  237.4 2.0 fusion.65
  241.9 14.9 %while.62 = (s32[]{:T(128)}, f32[512,128]{1,0:T(8,128)}, f32[512,128]{1,0:T(8,128)}, s32[]{:T(128)}, s32[512]{0:T(512)S(1)}, /*index=5*/s32[512]{0:T(512)S(1)}, ...) while((s32[]{:T(128)}, f32[512,128]{1,0:T(8,128)}, ...), condition=%wide.region_15.16_spmd.clone, body=%wide.region_12.15_spmd.clone.sunk | while | flops 4265478 | bytes 13388487 | solution.py:92
  242.0 3.0 gather_fusion.4
  245.7 4.4 fusion.109
  250.8 2.9 scatter_custom_fusion.50
  253.7 3.1 scatter_custom_fusion.51
  256.8 1.6 convert_element_type.93
  258.4 1.6 convert_element_type.95
  260.8 227.2 %all-reduce.10.cloned.1.call-done = (bf16[512,128]{1,0:T(8,128)(2,1)}, bf16[512,128]{1,0:T(8,128)(2,1)}) async-done(((bf16[512,128]{1,0:T(8,128)(2,1)}, bf16[512,128]{1,0:T(8,128)(2,1)}), (bf16[512,128]{1,0:T(8,128)(2,1)}, bf16[512,128]{1,0:T(8,128)(2,1)})) %all-reduce.10.cloned.1.call-update) | async-done | bytes 262160 | tf_op jit(solution)/shard_map/psum | solution.py:98
  490.0 12.7 %while.63 = (s32[]{:T(128)}, f32[1024,128]{1,0:T(8,128)S(1)}, f32[1024,128]{1,0:T(8,128)}, s32[]{:T(128)}, s32[512]{0:T(512)S(1)}, /*index=5*/s32[512]{0:T(512)S...) while((s32[]{:T(128)}, f32[1024,128]{1,0:T(8,128)S(1)}, ...), condition=%wide.region_21.22_spmd.clone, body=%wide.region_18.21_spmd.clone.sunk | while | flops 4265478 | bytes 13912775 | solution.py:117
  490.1 3.0 gather_fusion.6
  493.8 3.4 fusion.114
  499.4 3.3 scatter_custom_fusion.55
  504.9 8.1 collective-permute-start
  513.0 1.9 collective-permute-start.1
  514.9 3.1 collective-permute-done.1
  518.1 2.0 collective-permute-start.2
  521.3 3.4 collective-permute-done.3
  527.9 113.9 %all-reduce.4 = (f32[]{:T(128)}, f32[]{:T(128)}) all-reduce(f32[]{:T(128)} %get-tuple-element.839, f32[]{:T(128)} %get-tuple-element.837), channel_id=1, replica_groups=mesh['gz'=8,'gx'=32] {'gz','gx'}, use_global_device_ids=true, to_apply=%region_23.24 | all-reduce | flops 2 | bytes 16 | tf_op jit(solution)/shard_map/psum | solution.py:123
  643.4 3.5 collective-permute-start.4
  647.0 1.9 collective-permute-start.5
  648.9 3.1 collective-permute-done.5
  654.8 3.6 collective-permute-done.7
  661.7 77.6 %psum.69 = f32[]{:T(128)} all-reduce(f32[]{:T(128)} %get-tuple-element.833), channel_id=1, replica_groups=mesh['gz'=8,'gx'=32] {'gz','gx'}, use_global_device_ids=true, to_apply=%region_27.28 | all-reduce | flops 1 | bytes 8 | tf_op jit(solution)/shard_map/psum | solution.py:132
  740.1 3.5 collective-permute-start.8
  743.6 1.9 collective-permute-start.9
  745.5 3.1 collective-permute-done.9
  751.6 3.4 collective-permute-done.11
  758.3 78.8 %psum.70 = f32[]{:T(128)} all-reduce(f32[]{:T(128)} %get-tuple-element.829), channel_id=1, replica_groups=mesh['gz'=8,'gx'=32] {'gz','gx'}, use_global_device_ids=true, to_apply=%region_29.30 | all-reduce | flops 1 | bytes 8 | tf_op jit(solution)/shard_map/psum | solution.py:132
  837.8 3.5 collective-permute-start.12
  841.3 1.9 collective-permute-start.13
  843.3 3.1 collective-permute-done.13
  849.2 3.6 collective-permute-done.15
  856.0 78.8 %psum.71 = f32[]{:T(128)} all-reduce(f32[]{:T(128)} %get-tuple-element.825), channel_id=1, replica_groups=mesh['gz'=8,'gx'=32] {'gz','gx'}, use_global_device_ids=true, to_apply=%region_31.32 | all-reduce | flops 1 | bytes 8 | tf_op jit(solution)/shard_map/psum | solution.py:132
  (103 shorter events, 49.9 us)
Async XLA Ops:
  6.5 10.1 %copy-start.1 = (f32[32,16,256]{2,1,0:T(8,128)S(1)}, f32[32,16,256]{2,1,0:T(8,128)}, u32[]{:S(2)}) copy-start(f32[32,16,256]{2,1,0:T(8,128)} %param.16) | copy-start | bytes 1572868
  6.5 209.8 %all-reduce.12.cloned.1.call-start = ((), (), s32[]{:S(2)}) async-start(), calls=%async_computation.1 | async-start | bytes 524288 | tf_op jit(solution)/shard_map/psum | solution.py:98
  14.3 2.6 copy-start.3
  14.3 2.6 copy-start.4
  14.3 3.4 copy-start
  33.4 454.6 %all-reduce.10.cloned.1.call-start = ((), (), s32[]{:S(2)}) async-start(), calls=%async_computation | async-start | bytes 524288 | tf_op jit(solution)/shard_map/psum | solution.py:98
  502.7 1.3 copy-start.2
  504.9 10.0 %collective-permute-start = (f32[1,16,256]{2,1,0:T(8,128)S(1)}, f32[1,16,256]{2,1,0:T(8,128)S(1)}, u32[]{:S(2)}, u32[]{:S(2)}) collective-permute-start(f32[1,16,256]{2,1,0:T(8,128)S(1)} %get-tuple-element.879), channel_id=1, source_target_pairs={{0,32},{32,64},{64,96},{96,128},{128,160},{160,192},{192,224},{1,3... | collective-permute-start | bytes 49160 | tf_op jit(solution)/shard_map/ppermute | solution.py:21
  513.0 5.1 collective-permute-start.1
  518.1 3.3 collective-permute-start.2
  520.0 4.7 collective-permute-start.3
  643.4 5.5 collective-permute-start.4
  647.0 5.1 collective-permute-start.5
  652.1 2.7 collective-permute-start.6
  653.5 4.9 collective-permute-start.7
  740.1 5.4 collective-permute-start.8
  743.6 5.1 collective-permute-start.9
  748.7 2.9 collective-permute-start.10
  750.1 4.9 collective-permute-start.11
  837.8 5.4 collective-permute-start.12
  841.3 5.1 collective-permute-start.13
  846.5 2.7 collective-permute-start.14
  847.9 4.9 collective-permute-start.15
Sparse Core Ops, SparseCore 0:
  33.6 182.7 all-reduce.11
  260.1 227.8 all-reduce.9
where the time goes:
time: 946 us; the launch traced here: 943 us
  waiting for transfers between devices  434 us (46%)
  blocking collectives  349 us (37%)
  other arithmetic  55.2 us (6%)
  starting transfers between devices  37.9 us (4%)
  local copies, waits for them, and re-layouts  28.9 us (3%)
  between operations  22.3 us (2%)
  matrix products  15.6 us (2%)
    psum x2, waiting for transfers between devices, body(): lax.psum(ray_sum.astype(jnp.bfloat16), 'gx').astype(jnp.float32)  408 us
    psum x3, blocking collectives, body(): slope_total = lax.psum(slope_part, ('gz', 'gx'))  235 us
    psum x1, blocking collectives, body(): change_total = lax.psum(change_part, ('gz', 'gx'))  114 us
    ppermute x8, waiting for transfers between devices, padded_2(): lax.ppermute(head, axis, [((i + 1) % count, i) for i in range(ends)])  26.5 us
    ppermute x8, starting transfers between devices, padded_2(): lax.ppermute(tail, axis, [(i, (i + 1) % count) for i in range(ends)])  24.8 us
  transfers between devices with their start and end apart: 18, of which 10 were waited for; matrix products, arithmetic and copies ran while one was open for 0% of the time, Pallas kernels for 0%

commit v1 on v0

--- a/solution.py
+++ b/solution.py
@@ -129,7 +129,7 @@
         if sweep_index == 0:
             slope_total = lax.psum(slope_part, ("gz", "gx"))
         else:
-            slope_total = lax.psum(slope_part, ("gz", "gx"))
+            slope_total = lax.psum(lax.psum(slope_part, "gx"), "gz")
         change_total, scale_now = (
             change_total,
             step_gain * jnp.sqrt(change_total) / jnp.sqrt(slope_total + norm_floor),

time: 946 us -> 975 us (1.031); the launches traced: 943 us -> 956 us
  blocking collectives: 349 us -> 364 us
    psum x3 -> x6, blocking collectives: 235 us -> 251 us  [body(): slope_total = lax.psum(lax.psum(slope_part, 'gx'), 'gz')]
where the time goes in v1:
time: 975 us; the launch traced here: 956 us
  waiting for transfers between devices  432 us (44%)
  blocking collectives  364 us (37%)
  other arithmetic  55.1 us (6%)
  starting transfers between devices  37.7 us (4%)
  local copies, waits for them, and re-layouts  28.8 us (3%)
  between operations  22.5 us (2%)
  matrix products  15.6 us (2%)
    psum x2, waiting for transfers between devices, body(): lax.psum(ray_sum.astype(jnp.bfloat16), 'gx').astype(jnp.float32)  407 us
    psum x6, blocking collectives, body(): slope_total = lax.psum(lax.psum(slope_part, 'gx'), 'gz')  251 us
    psum x1, blocking collectives, body(): change_total = lax.psum(change_part, ('gz', 'gx'))  114 us
    ppermute x8, waiting for transfers between devices, padded_2(): lax.ppermute(head, axis, [((i + 1) % count, i) for i in range(ends)])  25 us
    ppermute x8, starting transfers between devices, padded_2(): lax.ppermute(tail, axis, [(i, (i + 1) % count) for i in range(ends)])  23.6 us
  transfers between devices with their start and end apart: 18, of which 10 were waited for; matrix products, arithmetic and copies ran while one was open for 0% of the time, Pallas kernels for 0%

profile of v1, /device:TPU:1, one launch (start us, length us, event | category | flops | bytes accessed | tf_op | source)
XLA Modules:
  0.0 956.3 jit_solution(11946203479004918018)
XLA Ops:
  14.7 2.4 convert_reduce_fusion
  18.0 13.5 %while.60 = (s32[]{:T(128)}, f32[512,128]{1,0:T(8,128)S(1)}, f32[512,128]{1,0:T(8,128)}, s32[]{:T(128)}, s32[512]{0:T(512)S(1)}, /*index=5*/s32[512]{0:T(512)S(1...) while((s32[]{:T(128)}, f32[512,128]{1,0:T(8,128)S(1)}, ...), condition=%wide.region_4.5_spmd.clone, body=%wide.region_1.4_spmd.clone.sunk | while | flops 4265478 | bytes 13388487 | solution.py:92
  18.1 3.0 gather_fusion
  21.8 4.4 fusion.99
  28.4 3.1 scatter_custom_fusion.43
  36.2 180.4 %all-reduce.12.cloned.1.call-done = (bf16[512,128]{1,0:T(8,128)(2,1)}, bf16[512,128]{1,0:T(8,128)(2,1)}) async-done(((bf16[512,128]{1,0:T(8,128)(2,1)}, bf16[512,128]{1,0:T(8,128)(2,1)}), (bf16[512,128]{1,0:T(8,128)(2,1)}, bf16[512,128]{1,0:T(8,128)(2,1)})) %all-reduce.12.cloned.1.call-update) | async-done | bytes 262160 | tf_op jit(solution)/shard_map/psum | solution.py:98
  219.4 14.2 %while.61 = (s32[]{:T(128)}, f32[1024,128]{1,0:T(8,128)}, f32[1024,128]{1,0:T(8,128)}, s32[]{:T(128)}, s32[512]{0:T(512)S(1)}, /*index=5*/s32[512]{0:T(512)S(1)}...) while((s32[]{:T(128)}, f32[1024,128]{1,0:T(8,128)}, ...), condition=%wide.region_11.12_spmd.clone, body=%wide.region_8.11_spmd.clone.sunk | while | flops 4265478 | bytes 13912775 | solution.py:117
  219.5 3.0 gather_fusion.2
  223.2 3.4 fusion.104
  227.3 3.1 scatter_custom_fusion.46
  230.3 3.3 scatter_custom_fusion.47
  233.6 2.1 add_divide_fusion.1
  235.6 2.0 reshape.54
  237.6 2.0 fusion.65
  242.1 14.8 %while.62 = (s32[]{:T(128)}, f32[512,128]{1,0:T(8,128)}, f32[512,128]{1,0:T(8,128)}, s32[]{:T(128)}, s32[512]{0:T(512)S(1)}, /*index=5*/s32[512]{0:T(512)S(1)}, ...) while((s32[]{:T(128)}, f32[512,128]{1,0:T(8,128)}, ...), condition=%wide.region_15.16_spmd.clone, body=%wide.region_12.15_spmd.clone.sunk | while | flops 4265478 | bytes 13388487 | solution.py:92
  242.2 3.0 gather_fusion.4
  245.9 4.4 fusion.109
  250.9 2.9 scatter_custom_fusion.50
  253.8 3.1 scatter_custom_fusion.51
  260.9 226.7 %all-reduce.10.cloned.1.call-done = (bf16[512,128]{1,0:T(8,128)(2,1)}, bf16[512,128]{1,0:T(8,128)(2,1)}) async-done(((bf16[512,128]{1,0:T(8,128)(2,1)}, bf16[512,128]{1,0:T(8,128)(2,1)}), (bf16[512,128]{1,0:T(8,128)(2,1)}, bf16[512,128]{1,0:T(8,128)(2,1)})) %all-reduce.10.cloned.1.call-update) | async-done | bytes 262160 | tf_op jit(solution)/shard_map/psum | solution.py:98
  489.6 12.6 %while.63 = (s32[]{:T(128)}, f32[1024,128]{1,0:T(8,128)S(1)}, f32[1024,128]{1,0:T(8,128)}, s32[]{:T(128)}, s32[512]{0:T(512)S(1)}, /*index=5*/s32[512]{0:T(512)S...) while((s32[]{:T(128)}, f32[1024,128]{1,0:T(8,128)S(1)}, ...), condition=%wide.region_21.22_spmd.clone, body=%wide.region_18.21_spmd.clone.sunk | while | flops 4265478 | bytes 13912775 | solution.py:117
  489.7 3.0 gather_fusion.6
  493.4 3.4 fusion.114
  498.9 3.3 scatter_custom_fusion.55
  504.3 8.1 collective-permute-start
  512.4 1.9 collective-permute-start.1
  514.4 3.1 collective-permute-done.1
  517.5 2.0 collective-permute-start.2
  520.8 3.4 collective-permute-done.3
  527.5 113.6 %all-reduce.4 = (f32[]{:T(128)}, f32[]{:T(128)}) all-reduce(f32[]{:T(128)} %get-tuple-element.839, f32[]{:T(128)} %get-tuple-element.837), channel_id=1, replica_groups=mesh['gz'=8,'gx'=32] {'gz','gx'}, use_global_device_ids=true, to_apply=%region_23.24 | all-reduce | flops 2 | bytes 16 | tf_op jit(solution)/shard_map/psum | solution.py:123
  642.5 3.5 collective-permute-start.4
  646.1 1.9 collective-permute-start.5
  648.0 3.1 collective-permute-done.5
  653.9 3.6 collective-permute-done.7
  660.7 59.5 %psum.90 = f32[]{:T(128)} all-reduce(f32[]{:T(128)} %get-tuple-element.833), channel_id=1, replica_groups=mesh['gz'=8,'gx'=32] {'gx'}, use_global_device_ids=true, to_apply=%region_27.28 | all-reduce | flops 1 | bytes 8 | tf_op jit(solution)/shard_map/psum | solution.py:132
  720.2 26.3 %psum.91 = f32[]{:T(128)} all-reduce(f32[]{:T(128)} %psum.90), channel_id=1, replica_groups=mesh['gz'=8,'gx'=32] {'gz'}, use_global_device_ids=true, to_apply=%region_28.29 | all-reduce | flops 1 | bytes 8 | tf_op jit(solution)/shard_map/psum | solution.py:132
  749.2 2.4 collective-permute-start.9
  751.7 2.6 collective-permute-done.9
  757.2 3.1 collective-permute-done.11
  763.6 56.8 %psum.92 = f32[]{:T(128)} all-reduce(f32[]{:T(128)} %get-tuple-element.829), channel_id=1, replica_groups=mesh['gz'=8,'gx'=32] {'gx'}, use_global_device_ids=true, to_apply=%region_30.31 | all-reduce | flops 1 | bytes 8 | tf_op jit(solution)/shard_map/psum | solution.py:132
  820.4 25.6 %psum.93 = f32[]{:T(128)} all-reduce(f32[]{:T(128)} %psum.92), channel_id=1, replica_groups=mesh['gz'=8,'gx'=32] {'gz'}, use_global_device_ids=true, to_apply=%region_31.32 | all-reduce | flops 1 | bytes 8 | tf_op jit(solution)/shard_map/psum | solution.py:132
  846.7 1.9 collective-permute-start.12
  848.6 2.4 collective-permute-start.13
  851.1 2.6 collective-permute-done.13
  853.8 3.6 collective-permute-start.14
  858.7 3.4 collective-permute-done.15
  865.3 56.3 %psum.94 = f32[]{:T(128)} all-reduce(f32[]{:T(128)} %get-tuple-element.825), channel_id=1, replica_groups=mesh['gz'=8,'gx'=32] {'gx'}, use_global_device_ids=true, to_apply=%region_33.34 | all-reduce | flops 1 | bytes 8 | tf_op jit(solution)/shard_map/psum | solution.py:132
  921.6 26.2 %psum.95 = f32[]{:T(128)} all-reduce(f32[]{:T(128)} %psum.94), channel_id=1, replica_groups=mesh['gz'=8,'gx'=32] {'gz'}, use_global_device_ids=true, to_apply=%region_34.35 | all-reduce | flops 1 | bytes 8 | tf_op jit(solution)/shard_map/psum | solution.py:132
  (106 shorter events, 54.9 us)
Async XLA Ops:
  6.5 10.5 %copy-start.1 = (f32[32,16,256]{2,1,0:T(8,128)S(1)}, f32[32,16,256]{2,1,0:T(8,128)}, u32[]{:S(2)}) copy-start(f32[32,16,256]{2,1,0:T(8,128)} %param.16) | copy-start | bytes 1572868
  6.5 210.1 %all-reduce.12.cloned.1.call-start = ((), (), s32[]{:S(2)}) async-start(), calls=%async_computation.1 | async-start | bytes 524288 | tf_op jit(solution)/shard_map/psum | solution.py:98
  14.7 2.6 copy-start.3
  14.7 2.6 copy-start.4
  14.7 3.4 copy-start
  33.8 453.8 %all-reduce.10.cloned.1.call-start = ((), (), s32[]{:S(2)}) async-start(), calls=%async_computation | async-start | bytes 524288 | tf_op jit(solution)/shard_map/psum | solution.py:98
  502.2 1.3 copy-start.2
  504.3 10.0 %collective-permute-start = (f32[1,16,256]{2,1,0:T(8,128)S(1)}, f32[1,16,256]{2,1,0:T(8,128)S(1)}, u32[]{:S(2)}, u32[]{:S(2)}) collective-permute-start(f32[1,16,256]{2,1,0:T(8,128)S(1)} %get-tuple-element.879), channel_id=1, source_target_pairs={{0,32},{32,64},{64,96},{96,128},{128,160},{160,192},{192,224},{1,3... | collective-permute-start | bytes 49160 | tf_op jit(solution)/shard_map/ppermute | solution.py:21
  512.4 5.1 collective-permute-start.1
  517.5 3.3 collective-permute-start.2
  519.5 4.7 collective-permute-start.3
  642.5 5.5 collective-permute-start.4
  646.1 5.1 collective-permute-start.5
  651.2 2.7 collective-permute-start.6
  652.5 4.9 collective-permute-start.7
  747.3 4.3 collective-permute-start.8
  749.2 5.1 collective-permute-start.9
  754.3 2.8 collective-permute-start.10
  755.6 4.7 collective-permute-start.11
  846.7 4.3 collective-permute-start.12
  848.6 5.1 collective-permute-start.13
  853.8 4.9 collective-permute-start.14
  857.3 4.7 collective-permute-start.15
Sparse Core Ops, SparseCore 0:
  33.9 182.6 all-reduce.11
  260.3 227.3 all-reduce.9
